TPU v7x, 32 devices: a whole 2x2x4 slice. The times are simulated.
32 devices in a mesh: rep: 2 (over x), ctx: 16 (over z, y, core).
Axes of the slice: x: 2, y: 2, z: 4, core: 2. Of those that a mesh axis runs over, the one named last changes fastest.
Arguments:
- queries: bfloat16 [4096, 12288], P(('rep', 'ctx')), parts along dimension 0, may hold values from -8 to 8
- latents: bfloat16 [512, 576], P(('rep', 'ctx')), parts along dimension 0, may hold values from -8 to 8
- w_key: bfloat16 [64, 512, 128], P('ctx'), may hold values from -0.25 to 0.25
- w_value: bfloat16 [64, 512, 128], P('ctx'), may hold values from -0.25 to 0.25
Outputs:
- attended: bfloat16 [4096, 8192], P(('rep', 'ctx')), parts along dimension 0
There are 2 independent parts, one for each index of `rep`. A program takes and returns all parts, laid end to end along the dimension named above; an argument that names none is the same for every part. Nothing has to cross between parts.
All inputs are finite; a program needn't handle non-finite values.
Results may differ from a plain program's by a relative error of at most 0.0067.
Values may be sent and summed in bfloat16 or wider, within the bound.
A program may use at most 128 MiB of HBM per device.

v0:
```python
import math

import jax
import jax.numpy as jnp
from jax import lax
from jax.sharding import PartitionSpec as P


def expand_block(block_rows, w_key, w_value):
    latent_width = w_key.shape[1]
    latent_part = block_rows[:, :latent_width]
    rope_part = block_rows[:, latent_width:]
    keys_nope = jnp.einsum(
        "td,hde->hte", latent_part, w_key, preferred_element_type=jnp.float32
    ).astype(jnp.bfloat16)
    values_all = jnp.einsum(
        "td,hde->hte", latent_part, w_value, preferred_element_type=jnp.float32
    ).astype(jnp.bfloat16)
    heads_here = w_key.shape[0]
    rope_wide = jnp.broadcast_to(rope_part[None], (heads_here,) + rope_part.shape)
    keys_full = jnp.concatenate([keys_nope, rope_wide], axis=2)
    return (keys_full, values_all)


def attend_rows(state_in, block_rows, by_head, w_key, w_value, score_scale):
    run_max, run_total, run_acc = state_in
    keys_full, values_all = expand_block(block_rows, w_key, w_value)
    scores = (
        jnp.einsum("qhe,hte->hqt", by_head, keys_full, preferred_element_type=jnp.float32)
        * score_scale
    )
    new_max = jnp.maximum(run_max, jnp.max(scores, axis=2))
    shrink = jnp.exp(run_max - new_max)
    weights = jnp.exp(scores - new_max[:, :, None])
    new_total = run_total * shrink + jnp.sum(weights, axis=2)
    weighted = jnp.einsum(
        "hqt,hte->qhe", weights.astype(jnp.bfloat16), values_all, preferred_element_type=jnp.float32
    )
    new_acc = run_acc * jnp.transpose(shrink)[:, :, None] + weighted
    return (new_max, new_total, new_acc)


def attend_piece(state_in, piece_rows, by_head, w_key, w_value, score_scale):
    row_count = piece_rows.shape[0]
    step_rows = math.gcd(row_count, 512)
    if step_rows == row_count:
        return attend_rows(state_in, piece_rows, by_head, w_key, w_value, score_scale)
    blocks = piece_rows.reshape(row_count // step_rows, step_rows, piece_rows.shape[1])

    def one_block(state_now, block_rows):
        return (attend_rows(state_now, block_rows, by_head, w_key, w_value, score_scale), None)

    state_out, unused = lax.scan(one_block, state_in, blocks)
    return state_out


def on_device(queries, latents, w_key, w_value):
    cycle_size = lax.axis_size("ctx")
    heads_here = w_key.shape[0]
    heads_all = heads_here * cycle_size
    query_rows = queries.shape[0]
    qk_width = queries.shape[1] // heads_all
    value_width = w_value.shape[2]
    score_scale = 1.0 / math.sqrt(qk_width)
    shaped = queries.reshape(query_rows, heads_all, qk_width)
    by_head = lax.all_to_all(shaped, "ctx", split_axis=1, concat_axis=0, tiled=True)
    positions = by_head.shape[0]
    start_state = (
        jnp.full((heads_here, positions), -jnp.inf, jnp.float32),
        jnp.zeros((heads_here, positions), jnp.float32),
        jnp.zeros((positions, heads_here, value_width), jnp.float32),
    )
    final_state = attend_piece(
        start_state,
        lax.all_gather(latents, "ctx", axis=0, tiled=True),
        by_head,
        w_key,
        w_value,
        score_scale,
    )
    run_max, run_total, run_acc = final_state
    attended = (run_acc / jnp.transpose(run_total)[:, :, None]).astype(jnp.bfloat16)
    returned = lax.all_to_all(attended, "ctx", split_axis=0, concat_axis=1, tiled=True)
    return returned.reshape(returned.shape[0], heads_all * value_width)


def solution(mesh):
    return jax.shard_map(
        on_device,
        mesh=mesh,
        in_specs=(
            P(("rep", "ctx"), None),
            P(("rep", "ctx"), None),
            P("ctx", None, None),
            P("ctx", None, None),
        ),
        out_specs=P(("rep", "ctx"), None),
        check_vma=False,
    )
```

profile of v0, /device:TPU:1, one launch (start us, length us, event | category | flops | bytes accessed | tf_op | source)
XLA Modules:
  0.0 166.1 jit_solution(692971591954095658)
XLA Ops:
  0.0 0.0 copy-start
  0.0 4.7 %copy.15 = bf16[128,12288]{0,1:T(8,128)(2,1)} copy(bf16[128,12288]{1,0:T(8,128)(2,1)} %param.4) | data formatting | bytes 6291456 | tf_op args[0]
  4.7 0.0 copy-start.2
  4.7 0.0 copy-start.3
  4.7 7.5 %all-to-all-start = ((bf16[128,64,192]{0,2,1:T(8,128)(2,1)}), bf16[128,64,192]{0,2,1:T(8,128)(2,1)}, u32[]{:S(2)}, u32[]{:S(2)}) async-start(bf16[128,64,192]{0,2,1:T(8,128)(2,1)} %bitcast.46), calls=%async_computation | async-start | bytes 6291456 | tf_op jit(solution)/shard_map/all_to_all | solution.py:66
  12.2 0.0 copy-done.2
  12.2 68.5 %all_gather.3 = bf16[256,576]{1,0:T(8,128)(2,1)S(1)} all-gather(bf16[16,576]{1,0:T(8,128)(2,1)S(1)} %copy-done.2), channel_id=1, replica_groups=mesh['rep'=2,'ctx'=16] {'ctx'}, dimensions={0}, use_global_device_ids=true | all-gather | bytes 313344 | tf_op jit(solution)/shard_map/all_gather | solution.py:75
  80.8 0.1 copy.14
  80.9 0.0 copy-done.3
  80.9 0.3 fusion.14
  81.2 0.0 all-to-all-done
  81.2 3.2 %bitcast_reduce_fusion = (f32[4,2048]{1,0:T(4,128)S(1)}, f32[4,256,2048]{2,1,0:T(8,128)S(1)}) fusion(bf16[16,4,24,8,128]{4,3,2,1,0:T(8,128)(2,1)} %bitcast.13, bf16[4,256,64]{1,2,0:T(8,128)(2,1)S(1)} %broadcast_in_dim.7, bf16[4,256,128]{1,2,0:T(8,128)(2,1)S(1)} %fusion.14), kind=kOutput, calls=%fused_computation.1 | convolution fusion | flops 810278912 | bytes 11960320 | tf_op jit(solution)/shard_map/qhe,hte->hqt/dot_general | solution.py:29
  84.5 0.0 copy-start.1
  84.5 1.5 fusion.1
  86.0 1.7 %copy-done.1 = f32[4,256,2048]{2,1,0:T(8,128)} copy-done((f32[4,256,2048]{2,1,0:T(8,128)}, f32[4,256,2048]{2,1,0:T(8,128)S(1)}, u32[]{:S(2)}) %copy-start.1) | copy-done | bytes 8388632
  87.7 0.0 copy-done
  87.7 6.9 %fusion.6 = bf16[2048,4,128]{0,2,1:T(8,128)(2,1)} fusion(f32[2048,4]{0,1:T(4,128)S(1)} %bitcast_add_fusion.1, f32[2048,4]{0,1:T(4,128)S(1)} %multiply_bitcast_fusion, f32[4,256,2048]{2,1,0:T(8,128)} %copy-done.1, f32[4,2048]{1,0:T(4,128)S(1)} %get-tuple-element.5, bf16[4,512,128]{2,1,0:T(8,128)(2,1)S(1)} %copy-done, bf16[256,576]{1,0:T(8,128)(2,1)S(1)} %all_gather.3), kind=kOutput, calls=%fused_computation.8 | convolution fusion | flops 680656896 | bytes 11370496 | tf_op jit(solution)/shard_map/hqt,hte->qhe/dot_general | solution.py:36
  94.6 3.1 %copy.19 = bf16[2048,4,128]{2,1,0:T(4,128)(2,1)S(1)} copy(bf16[2048,4,128]{0,2,1:T(8,128)(2,1)} %fusion.6) | data formatting | bytes 4194304 | tf_op jit(solution)/shard_map/convert_element_type | solution.py:82
  97.7 64.4 %all_to_all.33 = bf16[2048,4,128]{2,1,0:T(4,128)(2,1)S(1)} all-to-all(bf16[2048,4,128]{2,1,0:T(4,128)(2,1)S(1)} %copy.19), channel_id=1, replica_groups=mesh['rep'=2,'ctx'=16] {'ctx'}, dimensions={0} | all-to-all | bytes 4194304 | tf_op jit(solution)/shard_map/all_to_all | solution.py:83
  162.1 1.2 copy.20
  163.3 2.8 %reshape.12 = bf16[128,8192]{1,0:T(8,128)(2,1)} reshape(bf16[128,16,4,128]{3,2,1,0:T(4,128)(2,1)S(1)} %copy.20) | data formatting | bytes 4194304 | tf_op jit(solution)/shard_map/reshape | solution.py:84
  (4 shorter events, 0.1 us)
Async XLA Ops:
  0.0 87.7 %copy-start = (bf16[4,512,128]{2,1,0:T(8,128)(2,1)S(1)}, bf16[4,512,128]{2,1,0:T(8,128)(2,1)}, u32[]{:S(2)}) copy-start(bf16[4,512,128]{2,1,0:T(8,128)(2,1)} %param.7) | copy-start | bytes 1572868
  4.7 7.5 %copy-start.2 = (bf16[16,576]{1,0:T(8,128)(2,1)S(1)}, bf16[16,576]{1,0:T(8,128)(2,1)}, u32[]{:S(2)}) copy-start(bf16[16,576]{1,0:T(8,128)(2,1)} %param.5) | copy-start | bytes 55300
  4.7 76.1 %copy-start.3 = (bf16[4,512,128]{2,1,0:T(8,128)(2,1)S(1)}, bf16[4,512,128]{2,1,0:T(8,128)(2,1)}, u32[]{:S(2)}) copy-start(bf16[4,512,128]{2,1,0:T(8,128)(2,1)} %param.6) | copy-start | bytes 1572868
  4.7 76.5 %all-to-all-start = ((bf16[128,64,192]{0,2,1:T(8,128)(2,1)}), bf16[128,64,192]{0,2,1:T(8,128)(2,1)}, u32[]{:S(2)}, u32[]{:S(2)}) async-start(bf16[128,64,192]{0,2,1:T(8,128)(2,1)} %bitcast.46), calls=%async_computation | async-start | bytes 6291456 | tf_op jit(solution)/shard_map/all_to_all | solution.py:66
  84.5 3.2 %copy-start.1 = (f32[4,256,2048]{2,1,0:T(8,128)}, f32[4,256,2048]{2,1,0:T(8,128)S(1)}, u32[]{:S(2)}) copy-start(f32[4,256,2048]{2,1,0:T(8,128)S(1)} %get-tuple-element.6) | copy-start | bytes 25165828
where the time goes:
time: 166 us
  blocking collectives  133 us (80%)
  local copies, waits for them, and re-layouts  13.6 us (8%)
  matrix products  10.4 us (6%)
  starting transfers between devices  7.47 us (4%)
    all_gather x1, blocking collectives, on_device(): lax.all_gather(latents, 'ctx', axis=0, tiled=True)  68.5 us
    all_to_all x1, blocking collectives, on_device(): lax.all_to_all(attended, 'ctx', split_axis=0, concat_axis=1, tiled=True)  64.4 us
    all_to_all x1, starting transfers between devices, on_device(): lax.all_to_all(shaped, 'ctx', split_axis=1, concat_axis=0, tiled=True)  7.47 us
    dot_general x1, matrix products, attend_rows(): jnp.einsum('hqt,hte->qhe', weights.astype(jnp.bfloat16), values_all, pref...  6.86 us
    unnamed x9, local copies, waits for them, and re-layouts  6.46 us
  transfers between devices with their start and end apart: 1, of which 0 were waited for; matrix products, arithmetic and copies ran while one was open for 0% of the time, Pallas kernels for 0%

commit v1 on v0

v1 whole, which is shorter than its diff:
```python
import functools
import math

import jax
import jax.numpy as jnp
from jax import lax
from jax.experimental import pallas as pl
from jax.experimental.pallas import tpu as pltpu
from jax.sharding import PartitionSpec as P

MESH = pl.DeviceIdType.MESH


def kernel(
    grid_y,
    cores,
    q_hbm,
    lat_hbm,
    wk_hbm,
    wv_hbm,
    out_hbm,
    q,
    lat,
    wkv,
    ropes,
    kv,
    o,
    load_sem,
    out_sem,
    lat_recv,
    lat_send,
    lat_relay,
    kv_recv,
    kv_right,
    kv_left,
    kv_across,
):
    devices = kv.shape[0]
    heads = kv.shape[1]
    rows = kv.shape[3]
    nope = kv.shape[4]
    block = lat.shape[1]
    width = wkv.shape[1]
    rope = lat.shape[2] - width
    qk = nope + rope
    chips = devices // cores
    grid_z = chips // grid_y
    half = chips // 2
    scale = math.log2(math.e) / math.sqrt(qk)

    me = lax.axis_index("ctx")
    core = lax.rem(me, cores)
    my_chip = me // cores
    my_y = lax.rem(my_chip, grid_y)
    my_z = my_chip // grid_y
    place = (1 - my_y) * my_z + my_y * (2 * grid_z - 1 - my_z)

    def device_at(spot, which):
        spot = lax.rem(spot + 2 * chips, chips)
        y = spot // grid_z
        z = (1 - y) * spot + y * (2 * grid_z - 1 - spot)
        return (z * grid_y + y) * cores + which

    other_core = cores - 1 - core
    across = my_chip * cores + other_core
    right = device_at(place + 1, core)
    left = device_at(place - 1, core)

    q_copy = pltpu.make_async_copy(q_hbm, q, load_sem.at[0])
    lat_copy = pltpu.make_async_copy(lat_hbm, lat.at[me], load_sem.at[1])
    lat_copy.start()
    w_copies = []
    for j in range(heads):
        w_copies.append(
            pltpu.make_async_copy(wk_hbm.at[j], wkv.at[j, :, pl.ds(0, nope)], load_sem.at[2 + 2 * j])
        )
        w_copies.append(
            pltpu.make_async_copy(wv_hbm.at[j], wkv.at[j, :, pl.ds(nope, nope)], load_sem.at[3 + 2 * j])
        )
    for copy in w_copies:
        copy.start()
    q_copy.start()

    barrier = pltpu.get_barrier_semaphore()

    @pl.loop(1, chips)
    def _(d):
        pl.semaphore_signal(
            barrier, inc=1, device_id={"ctx": device_at(place + d, core)}, device_id_type=MESH
        )

    pl.semaphore_signal(barrier, inc=1, device_id={"ctx": across}, device_id_type=MESH)
    pl.semaphore_wait(barrier, chips)

    def lat_out(d):
        return pltpu.make_async_remote_copy(
            src_ref=lat_hbm,
            dst_ref=lat.at[me],
            send_sem=lat_send.at[d],
            recv_sem=lat_recv.at[me],
            device_id={"ctx": device_at(place + d, core)},
            device_id_type=MESH,
        )

    def lat_on(owner):
        return pltpu.make_async_remote_copy(
            src_ref=lat.at[owner],
            dst_ref=lat.at[owner],
            send_sem=lat_relay.at[owner],
            recv_sem=lat_recv.at[owner],
            device_id={"ctx": across},
            device_id_type=MESH,
        )

    @pl.loop(1, chips)
    def _(d):
        lat_out(chips - d).start()

    lat_copy.wait()
    lat_on(me).start()

    @pl.loop(1, chips)
    def _(d):
        owner = device_at(place + d, core)
        lat_on(owner).wait_recv()
        lat_on(owner).start()

    @pl.loop(0, chips)
    def _(d):
        lat_on(device_at(place + d, other_core)).wait_recv()

    for copy in w_copies:
        copy.wait()

    lat_all = lat[...].reshape(rows, lat.shape[2])
    rope_part = lat_all[:, width:]
    blank = jnp.zeros_like(rope_part)
    ropes[0] = jnp.concatenate([rope_part, blank], axis=1)
    ropes[1] = jnp.concatenate([blank, rope_part], axis=1)

    def parity(owner, j):
        if heads % 2 == 0:
            return j % 2
        return lax.rem(owner * heads + j, 2)

    def send(owner, j, sems, target):
        return pltpu.make_async_remote_copy(
            src_ref=kv.at[owner, j],
            dst_ref=kv.at[owner, j],
            send_sem=sems.at[owner, j],
            recv_sem=kv_recv.at[owner, j],
            device_id={"ctx": target},
            device_id_type=MESH,
        )

    def go_right(owner, j):
        return send(owner, j, kv_right, right)

    def go_left(owner, j):
        return send(owner, j, kv_left, left)

    def go_across(owner, j):
        return send(owner, j, kv_across, across)

    half_right = (heads + 1) // 2
    for j in range(heads + 1):
        if j < heads:
            both = jnp.dot(lat_all[:, :width], wkv[j], preferred_element_type=jnp.float32)
            keys = both[:, :nope]
            odd = parity(me, j)
            turned = jnp.concatenate([keys[:, rope:], keys[:, :rope]], axis=1)
            if isinstance(odd, int):
                keys = turned if odd else keys
            else:
                keys = jnp.where(odd == 1, turned, keys)
            kv[me, j, 0] = keys.astype(jnp.bfloat16)
            kv[me, j, 1] = both[:, nope:].astype(jnp.bfloat16)
        if j > 0:
            go_right(me, j - 1).start()
            go_left(me, j - 1).start()
            go_across(me, j - 1).start()

    q_copy.wait()

    lane = lax.broadcasted_iota(jnp.int32, (rows, nope), 1)
    upper = lane >= rope

    def attend(owner, j):
        odd = parity(owner, j)
        head = owner * heads + j
        pair = owner * (heads // 2) + j // 2 if heads % 2 == 0 else head // 2
        start = pl.multiple_of(pair * (2 * qk) + odd * nope, nope)
        queries = q[:, pl.ds(start, 2 * nope)]
        keys = kv[owner, j, 0]

        def even_keys():
            return jnp.concatenate([keys, ropes[0]], axis=1)

        def odd_keys():
            return jnp.concatenate(
                [jnp.where(upper, keys, jnp.zeros_like(keys)), jnp.where(upper, ropes[1], keys)], axis=1
            )

        if isinstance(odd, int):
            keys_full = odd_keys() if odd else even_keys()
        else:
            keys_full = jnp.where(odd == 1, odd_keys(), even_keys())
        scores = lax.dot_general(
            queries, keys_full, (((1,), (1,)), ((), ())), preferred_element_type=jnp.float32
        )
        row_max = jnp.max(scores, axis=1, keepdims=True)
        weights = jnp.exp2((scores - row_max) * scale)
        total = jnp.sum(weights, axis=1, keepdims=True)
        mixed = jnp.dot(weights.astype(jnp.bfloat16), kv[owner, j, 1], preferred_element_type=jnp.float32)
        o[:, pl.ds(pl.multiple_of(head * nope, nope), nope)] = (mixed * (1.0 / total)).astype(jnp.bfloat16)

    def put(owner):
        columns = pl.ds(pl.multiple_of(owner * (heads * nope), nope), heads * nope)
        return pltpu.make_async_copy(o.at[:, columns], out_hbm.at[:, columns], out_sem.at[owner])

    def attend_other(owners, js):
        for j in js:
            for owner in owners:
                go_across(owner, j).wait_recv()
            for owner in owners:
                attend(owner, j)
        for owner in owners:
            put(owner).start()

    for j in range(heads):
        attend(me, j)
    put(me).start()

    def ring_step(s, fwd_right, fwd_left, before):
        from_left = device_at(place - s, core)
        from_right = device_at(place + s, core)
        for j in range(heads):
            go_right(from_left, j).wait_recv()
            if j < fwd_right:
                go_right(from_left, j).start()
            go_across(from_left, j).start()
            go_left(from_right, j).wait_recv()
            if j >= fwd_left:
                go_left(from_right, j).start()
            go_across(from_right, j).start()
            for owner in before:
                go_across(owner, j).wait_recv()
            attend(from_left, j)
            attend(from_right, j)
            for owner in before:
                attend(owner, j)
        put(from_left).start()
        put(from_right).start()
        for owner in before:
            put(owner).start()

    def others(s):
        return (device_at(place - s, other_core), device_at(place + s, other_core))

    if half > 1:
        first_right = heads if half > 2 else half_right
        first_left = 0 if half > 2 else half_right
        ring_step(1, first_right, first_left, (across,))
        if half > 3:

            @pl.loop(2, half - 1)
            def _(s):
                ring_step(s, heads, 0, others(s - 1))

        if half > 2:
            ring_step(half - 1, half_right, half_right, others(half - 2))

    far = device_at(place + half, core)
    far_other = device_at(place + half, other_core)
    last_before = others(half - 1) if half > 1 else (across,)
    order = []
    for j in range(half_right):
        order.append(j)
        if j + half_right < heads:
            order.append(j + half_right)
    for j in order:
        (go_right if j < half_right else go_left)(far, j).wait_recv()
        go_across(far, j).start()
        for owner in last_before:
            go_across(owner, j).wait_recv()
        for owner in last_before:
            attend(owner, j)
        attend(far, j)
    for owner in last_before:
        put(owner).start()
    put(far).start()
    attend_other((far_other,), order)

    @pl.loop(1, chips)
    def _(d):
        lat_out(d).wait_send()

    @pl.loop(0, chips)
    def _(d):
        owner = device_at(place + d, core)
        lat_on(owner).wait_send()
        for j in range(heads):
            go_across(owner, j).wait_send()

    @pl.loop(0, half - 1)
    def _(s):
        for j in range(heads):
            go_right(device_at(place - s, core), j).wait_send()
            go_left(device_at(place + s, core), j).wait_send()

    for j in range(heads):
        if j < half_right:
            go_right(device_at(place - (half - 1), core), j).wait_send()
        else:
            go_left(device_at(place + (half - 1), core), j).wait_send()

    @pl.loop(0, devices)
    def _(owner):
        put(owner).wait()


def on_device(grid_y, cores, queries, latents, w_key, w_value):
    devices = lax.axis_size("ctx")
    heads, width, nope = w_key.shape
    query_rows = queries.shape[0]
    block = latents.shape[0]
    rows = block * devices
    chips = devices // cores
    anywhere = pl.BlockSpec(memory_space=pl.ANY)
    dma = pltpu.SemaphoreType.DMA
    return pl.pallas_call(
        functools.partial(kernel, grid_y, cores),
        out_shape=jax.ShapeDtypeStruct((query_rows, devices * heads * nope), jnp.bfloat16),
        in_specs=[anywhere] * 4,
        out_specs=anywhere,
        scratch_shapes=[
            pltpu.VMEM(queries.shape, jnp.bfloat16),
            pltpu.VMEM((devices, block, latents.shape[1]), jnp.bfloat16),
            pltpu.VMEM((heads, width, 2 * nope), jnp.bfloat16),
            pltpu.VMEM((2, rows, nope), jnp.bfloat16),
            pltpu.VMEM((devices, heads, 2, rows, nope), jnp.bfloat16),
            pltpu.VMEM((query_rows, devices * heads * nope), jnp.bfloat16),
            dma((2 + 2 * heads,)),
            dma((devices,)),
            dma((devices,)),
            dma((chips,)),
            dma((devices,)),
            dma((devices, heads)),
            dma((devices, heads)),
            dma((devices, heads)),
            dma((devices, heads)),
        ],
        compiler_params=pltpu.CompilerParams(
            collective_id=0, has_side_effects=True, vmem_limit_bytes=56 * 1024 * 1024
        ),
    )(queries, latents, w_key, w_value)


def layout_of(mesh):
    group = list(mesh.devices.reshape(-1, mesh.shape["ctx"])[0])
    places = [tuple(d.coords) for d in group]
    chips = sorted(set(places))
    cores = len(group) // len(chips)
    varied = [axis for axis in range(3) if len({c[axis] for c in chips}) > 1]
    grid_y = 1
    if len(varied) == 2:
        fast = len({c[varied[0]] for c in chips})
        grid_y = 2 if fast == 2 else 1
    return grid_y, cores


def solution(mesh):
    grid_y, cores = layout_of(mesh)
    return jax.shard_map(
        functools.partial(on_device, grid_y, cores),
        mesh=mesh,
        in_specs=(
            P(("rep", "ctx"), None),
            P(("rep", "ctx"), None),
            P("ctx", None, None),
            P("ctx", None, None),
        ),
        out_specs=P(("rep", "ctx"), None),
        check_vma=False,
    )
```

time: 166 us -> 63.4 us (0.38)
  blocking collectives: 133 us -> 0 us
  Pallas kernels: 0 us -> 60 us
  local copies, waits for them, and re-layouts: 13.6 us -> 3.1 us
  matrix products: 10.4 us -> 0 us
  starting transfers between devices: 7.47 us -> 0 us
    all_gather x1 -> x0, blocking collectives: 68.5 us -> none  [on_device(): lax.all_gather(latents, 'ctx', axis=0, tiled=True)]
    all_to_all x1 -> x0, blocking collectives: 64.4 us -> none  [on_device(): lax.all_to_all(attended, 'ctx', split_axis=0, concat_axis=1, tiled=True)]
    pallas_call x0 -> x1, Pallas kernels: none -> 60 us  [on_device(): pl.pallas_call(functools.partial(kernel, grid_y, cores), out_shape=jax.Sh...]
    dot_general x3 -> x0, matrix products: 10.4 us -> none  [the longest x1 6.86 us: attend_rows(): jnp.einsum('hqt,hte->qhe', weights.astype(jnp.bfloat16), values_all, pref...]
    all_to_all x1 -> x0, starting transfers between devices: 7.47 us -> none  [on_device(): lax.all_to_all(shaped, 'ctx', split_axis=1, concat_axis=0, tiled=True)]
    unnamed x9 -> x1, local copies, waits for them, and re-layouts: 6.46 us -> 3.1 us
    convert_element_type x1 -> x0, local copies, waits for them, and re-layouts: 3.09 us -> none  [on_device(): (run_acc / jnp.transpose(run_total)[:, :, None]).astype(jnp.bfloat16)]
    reshape x1 -> x0, local copies, waits for them, and re-layouts: 2.8 us -> none  [on_device(): return returned.reshape(returned.shape[0], heads_all * value_width)]
  transfers between devices with their start and end apart: 1 -> 0, of which waited for: 0 -> 0; matrix products, arithmetic and copies ran while one was open for 0% -> 0% of each run, Pallas kernels for 0% -> 0%
where the time goes in v1:
time: 63.4 us; the launch traced here: 63.1 us
  Pallas kernels  60 us (95%)
  local copies, waits for them, and re-layouts  3.1 us (5%)
    pallas_call x1, Pallas kernels, on_device(): pl.pallas_call(functools.partial(kernel, grid_y, cores), out_shape=jax.Sh...  60 us
    unnamed x1, local copies, waits for them, and re-layouts  3.1 us

profile of v1, /device:TPU:1, one launch (start us, length us, event | category | flops | bytes accessed | tf_op | source)
XLA Modules:
  0.0 63.1 jit_solution(16218430675531856114)
XLA Ops:
  0.0 60.0 %shard_map.46 = bf16[128,8192]{1,0:T(8,128)(2,1)} custom-call(bf16[128,12288]{1,0:T(8,128)(2,1)} %q_hbm.1, bf16[16,576]{1,0:T(8,128)(2,1)} %lat_hbm.1, bf16[4,512,128]{2,1,0:T(8,128)(2,1)} %wk_hbm.1, bf16[4,512,128]{2,1,0:T(8,128)(2,1)} %wv_hbm.1), custom_call_target="tpu_custom_call" | custom-call | tf_op jit(solution)/shard_map/pallas_call | solution.py:331
  60.0 3.1 %copy.6 = bf16[128,8192]{1,0:T(8,128)(2,1)} copy(bf16[128,8192]{1,0:T(8,128)(2,1)} %shard_map.46) | data formatting | bytes 4194304

commit v2 on v1

--- a/solution.py
+++ b/solution.py
@@ -18,15 +18,13 @@
     lat_hbm,
     wk_hbm,
     wv_hbm,
-    out_hbm,
+    o,
     q,
     lat,
     wkv,
     ropes,
     kv,
-    o,
     load_sem,
-    out_sem,
     lat_recv,
     lat_send,
     lat_relay,
@@ -214,22 +212,15 @@
         mixed = jnp.dot(weights.astype(jnp.bfloat16), kv[owner, j, 1], preferred_element_type=jnp.float32)
         o[:, pl.ds(pl.multiple_of(head * nope, nope), nope)] = (mixed * (1.0 / total)).astype(jnp.bfloat16)
 
-    def put(owner):
-        columns = pl.ds(pl.multiple_of(owner * (heads * nope), nope), heads * nope)
-        return pltpu.make_async_copy(o.at[:, columns], out_hbm.at[:, columns], out_sem.at[owner])
-
     def attend_other(owners, js):
         for j in js:
             for owner in owners:
                 go_across(owner, j).wait_recv()
             for owner in owners:
                 attend(owner, j)
-        for owner in owners:
-            put(owner).start()
 
     for j in range(heads):
         attend(me, j)
-    put(me).start()
 
     def ring_step(s, fwd_right, fwd_left, before):
         from_left = device_at(place - s, core)
@@ -249,10 +240,6 @@
             attend(from_right, j)
             for owner in before:
                 attend(owner, j)
-        put(from_left).start()
-        put(from_right).start()
-        for owner in before:
-            put(owner).start()
 
     def others(s):
         return (device_at(place - s, other_core), device_at(place + s, other_core))
@@ -286,9 +273,6 @@
         for owner in last_before:
             attend(owner, j)
         attend(far, j)
-    for owner in last_before:
-        put(owner).start()
-    put(far).start()
     attend_other((far_other,), order)
 
     @pl.loop(1, chips)
@@ -313,10 +297,6 @@
             go_right(device_at(place - (half - 1), core), j).wait_send()
         else:
             go_left(device_at(place + (half - 1), core), j).wait_send()
-
-    @pl.loop(0, devices)
-    def _(owner):
-        put(owner).wait()
 
 
 def on_device(grid_y, cores, queries, latents, w_key, w_value):
@@ -332,16 +312,14 @@
         functools.partial(kernel, grid_y, cores),
         out_shape=jax.ShapeDtypeStruct((query_rows, devices * heads * nope), jnp.bfloat16),
         in_specs=[anywhere] * 4,
-        out_specs=anywhere,
+        out_specs=pl.BlockSpec(memory_space=pltpu.VMEM),
         scratch_shapes=[
             pltpu.VMEM(queries.shape, jnp.bfloat16),
             pltpu.VMEM((devices, block, latents.shape[1]), jnp.bfloat16),
             pltpu.VMEM((heads, width, 2 * nope), jnp.bfloat16),
             pltpu.VMEM((2, rows, nope), jnp.bfloat16),
             pltpu.VMEM((devices, heads, 2, rows, nope), jnp.bfloat16),
-            pltpu.VMEM((query_rows, devices * heads * nope), jnp.bfloat16),
             dma((2 + 2 * heads,)),
-            dma((devices,)),
             dma((devices,)),
             dma((chips,)),
             dma((devices,)),
@@ -351,7 +329,7 @@
             dma((devices, heads)),
         ],
         compiler_params=pltpu.CompilerParams(
-            collective_id=0, has_side_effects=True, vmem_limit_bytes=56 * 1024 * 1024
+            collective_id=0, has_side_effects=True, vmem_limit_bytes=50 * 1024 * 1024
         ),
     )(queries, latents, w_key, w_value)
 

time: 63.4 us -> 64.1 us (1.011)
  local copies, waits for them, and re-layouts: 3.1 us -> 4.13 us
    unnamed x1 -> x7, local copies, waits for them, and re-layouts: 3.1 us -> 4.13 us
where the time goes in v2:
time: 64.1 us; the launch traced here: 63.7 us
  Pallas kernels  59.6 us (93%)
  local copies, waits for them, and re-layouts  4.13 us (6%)
    pallas_call x1, Pallas kernels, on_device(): pl.pallas_call(functools.partial(kernel, grid_y, cores), out_shape=jax.Sh...  59.6 us
    unnamed x7, local copies, waits for them, and re-layouts  4.13 us

profile of v2, /device:TPU:1, one launch (start us, length us, event | category | flops | bytes accessed | tf_op | source)
XLA Modules:
  0.0 63.7 jit_solution(9896005545300584548)
XLA Ops:
  0.0 0.0 copy-start
  0.0 1.0 %copy-done = bf16[4,512,128]{2,1,0:T(8,128)(2,1)S(1)} copy-done((bf16[4,512,128]{2,1,0:T(8,128)(2,1)S(1)}, bf16[4,512,128]{2,1,0:T(8,128)(2,1)}, u32[]{:S(2)}) %copy-start) | copy-done | bytes 524312
  1.0 0.0 copy-start.1
  1.0 1.0 %copy-done.1 = bf16[4,512,128]{2,1,0:T(8,128)(2,1)S(1)} copy-done((bf16[4,512,128]{2,1,0:T(8,128)(2,1)S(1)}, bf16[4,512,128]{2,1,0:T(8,128)(2,1)}, u32[]{:S(2)}) %copy-start.1) | copy-done | bytes 524312
  2.1 0.0 copy-start.2
  2.1 0.7 %copy-done.2 = bf16[16,576]{1,0:T(8,128)(2,1)S(1)} copy-done((bf16[16,576]{1,0:T(8,128)(2,1)S(1)}, bf16[16,576]{1,0:T(8,128)(2,1)}, u32[]{:S(2)}) %copy-start.2) | copy-done | bytes 18456
  2.8 59.6 %shard_map.46 = bf16[128,8192]{1,0:T(8,128)(2,1)S(1)} custom-call(bf16[128,12288]{1,0:T(8,128)(2,1)} %q_hbm.1, bf16[16,576]{1,0:T(8,128)(2,1)S(1)} %copy-done.2, bf16[4,512,128]{2,1,0:T(8,128)(2,1)S(1)} %copy-done, bf16[4,512,128]{2,1,0:T(8,128)(2,1)S(1)} %copy-done.1), custom_call_target="tpu_custom_call" | custom-call | tf_op jit(solution)/shard_map/pallas_call | solution.py:311
  62.4 1.3 %copy.6 = bf16[128,8192]{1,0:T(8,128)(2,1)} copy(bf16[128,8192]{1,0:T(8,128)(2,1)S(1)} %shard_map.46) | data formatting | bytes 4194304
Async XLA Ops:
  0.0 1.0 %copy-start = (bf16[4,512,128]{2,1,0:T(8,128)(2,1)S(1)}, bf16[4,512,128]{2,1,0:T(8,128)(2,1)}, u32[]{:S(2)}) copy-start(bf16[4,512,128]{2,1,0:T(8,128)(2,1)} %wk_hbm.1) | copy-start | bytes 1572868
  1.0 1.0 %copy-start.1 = (bf16[4,512,128]{2,1,0:T(8,128)(2,1)S(1)}, bf16[4,512,128]{2,1,0:T(8,128)(2,1)}, u32[]{:S(2)}) copy-start(bf16[4,512,128]{2,1,0:T(8,128)(2,1)} %wv_hbm.1) | copy-start | bytes 1572868
  2.1 0.7 %copy-start.2 = (bf16[16,576]{1,0:T(8,128)(2,1)S(1)}, bf16[16,576]{1,0:T(8,128)(2,1)}, u32[]{:S(2)}) copy-start(bf16[16,576]{1,0:T(8,128)(2,1)} %lat_hbm.1) | copy-start | bytes 55300

commit v3 on v2

--- a/solution.py
+++ b/solution.py
@@ -35,8 +35,8 @@
 ):
     devices = kv.shape[0]
     heads = kv.shape[1]
-    rows = kv.shape[3]
-    nope = kv.shape[4]
+    rows = 2 * kv.shape[4]
+    nope = kv.shape[5]
     block = lat.shape[1]
     width = wkv.shape[1]
     rope = lat.shape[2] - width
@@ -90,13 +90,22 @@
     pl.semaphore_signal(barrier, inc=1, device_id={"ctx": across}, device_id_type=MESH)
     pl.semaphore_wait(barrier, chips)
 
-    def lat_out(d):
+    near = me // (devices // 2)
+    chips_half = chips // 2
+
+    def near_chip(i):
+        return near * chips_half + lax.rem(my_chip - near * chips_half + i, chips_half)
+
+    def far_chip(i):
+        return (1 - near) * chips_half + lax.rem(my_chip - near * chips_half + i, chips_half)
+
+    def lat_out(chip):
         return pltpu.make_async_remote_copy(
             src_ref=lat_hbm,
             dst_ref=lat.at[me],
-            send_sem=lat_send.at[d],
+            send_sem=lat_send.at[chip],
             recv_sem=lat_recv.at[me],
-            device_id={"ctx": device_at(place + d, core)},
+            device_id={"ctx": chip * cores + core},
             device_id_type=MESH,
         )
 
@@ -110,73 +119,105 @@
             device_id_type=MESH,
         )
 
-    @pl.loop(1, chips)
-    def _(d):
-        lat_out(chips - d).start()
+    @pl.loop(1, chips_half)
+    def _(i):
+        lat_out(near_chip(i)).start()
+
+    @pl.loop(0, chips_half)
+    def _(i):
+        lat_out(far_chip(i)).start()
 
     lat_copy.wait()
     lat_on(me).start()
 
-    @pl.loop(1, chips)
-    def _(d):
-        owner = device_at(place + d, core)
+    def relay(chip):
+        owner = chip * cores + core
         lat_on(owner).wait_recv()
         lat_on(owner).start()
 
-    @pl.loop(0, chips)
-    def _(d):
-        lat_on(device_at(place + d, other_core)).wait_recv()
+    @pl.loop(1, chips_half)
+    def _(i):
+        relay(near_chip(i))
+
+    @pl.loop(0, chips_half)
+    def _(i):
+        lat_on(near_chip(i) * cores + other_core).wait_recv()
 
     for copy in w_copies:
         copy.wait()
-
-    lat_all = lat[...].reshape(rows, lat.shape[2])
-    rope_part = lat_all[:, width:]
-    blank = jnp.zeros_like(rope_part)
-    ropes[0] = jnp.concatenate([rope_part, blank], axis=1)
-    ropes[1] = jnp.concatenate([blank, rope_part], axis=1)
 
     def parity(owner, j):
         if heads % 2 == 0:
             return j % 2
         return lax.rem(owner * heads + j, 2)
 
-    def send(owner, j, sems, target):
+    def send(owner, j, part, sems, target):
+        return pltpu.make_async_remote_copy(
+            src_ref=kv.at[owner, j, part],
+            dst_ref=kv.at[owner, j, part],
+            send_sem=sems.at[owner, j, part],
+            recv_sem=kv_recv.at[owner, j, part],
+            device_id={"ctx": target},
+            device_id_type=MESH,
+        )
+
+    def first_part(owner):
+        return owner // (devices // 2)
+
+    def go_right(owner, j, part):
+        return send(owner, j, part, kv_right, right)
+
+    def go_left(owner, j, part):
+        return send(owner, j, part, kv_left, left)
+
+    def go_across(owner, j):
         return pltpu.make_async_remote_copy(
             src_ref=kv.at[owner, j],
             dst_ref=kv.at[owner, j],
-            send_sem=sems.at[owner, j],
-            recv_sem=kv_recv.at[owner, j],
-            device_id={"ctx": target},
+            send_sem=kv_across.at[owner, j],
+            recv_sem=kv_recv.at[owner, j, 0],
+            device_id={"ctx": across},
             device_id_type=MESH,
         )
 
-    def go_right(owner, j):
-        return send(owner, j, kv_right, right)
-
-    def go_left(owner, j):
-        return send(owner, j, kv_left, left)
-
-    def go_across(owner, j):
-        return send(owner, j, kv_across, across)
-
     half_right = (heads + 1) // 2
-    for j in range(heads + 1):
-        if j < heads:
-            both = jnp.dot(lat_all[:, :width], wkv[j], preferred_element_type=jnp.float32)
-            keys = both[:, :nope]
-            odd = parity(me, j)
-            turned = jnp.concatenate([keys[:, rope:], keys[:, :rope]], axis=1)
-            if isinstance(odd, int):
-                keys = turned if odd else keys
-            else:
-                keys = jnp.where(odd == 1, turned, keys)
-            kv[me, j, 0] = keys.astype(jnp.bfloat16)
-            kv[me, j, 1] = both[:, nope:].astype(jnp.bfloat16)
-        if j > 0:
-            go_right(me, j - 1).start()
-            go_left(me, j - 1).start()
-            go_across(me, j - 1).start()
+
+    def project(part, last):
+        some = lat[pl.ds(part * (devices // 2), devices // 2)].reshape(rows // 2, lat.shape[2])
+        for j in range(heads + 1):
+            if j < heads:
+                both = jnp.dot(some[:, :width], wkv[j], preferred_element_type=jnp.float32)
+                keys = both[:, :nope]
+                odd = parity(me, j)
+                turned = jnp.concatenate([keys[:, rope:], keys[:, :rope]], axis=1)
+                if isinstance(odd, int):
+                    keys = turned if odd else keys
+                else:
+                    keys = jnp.where(odd == 1, turned, keys)
+                kv[me, j, part, 0] = keys.astype(jnp.bfloat16)
+                kv[me, j, part, 1] = both[:, nope:].astype(jnp.bfloat16)
+            if j > 0:
+                go_right(me, j - 1, part).start()
+                go_left(me, j - 1, part).start()
+                if last:
+                    go_across(me, j - 1).start()
+
+    project(near, False)
+
+    @pl.loop(0, chips_half)
+    def _(i):
+        relay(far_chip(i))
+
+    @pl.loop(0, chips_half)
+    def _(i):
+        lat_on(far_chip(i) * cores + other_core).wait_recv()
+
+    project(1 - near, True)
+
+    rope_part = lat[...].reshape(rows, lat.shape[2])[:, width:]
+    blank = jnp.zeros_like(rope_part)
+    ropes[0] = jnp.concatenate([rope_part, blank], axis=1)
+    ropes[1] = jnp.concatenate([blank, rope_part], axis=1)
 
     q_copy.wait()
 
@@ -189,7 +230,8 @@
         pair = owner * (heads // 2) + j // 2 if heads % 2 == 0 else head // 2
         start = pl.multiple_of(pair * (2 * qk) + odd * nope, nope)
         queries = q[:, pl.ds(start, 2 * nope)]
-        keys = kv[owner, j, 0]
+        keys = kv[owner, j, :, 0].reshape(rows, nope)
+        values = kv[owner, j, :, 1].reshape(rows, nope)
 
         def even_keys():
             return jnp.concatenate([keys, ropes[0]], axis=1)
@@ -209,7 +251,7 @@
         row_max = jnp.max(scores, axis=1, keepdims=True)
         weights = jnp.exp2((scores - row_max) * scale)
         total = jnp.sum(weights, axis=1, keepdims=True)
-        mixed = jnp.dot(weights.astype(jnp.bfloat16), kv[owner, j, 1], preferred_element_type=jnp.float32)
+        mixed = jnp.dot(weights.astype(jnp.bfloat16), values, preferred_element_type=jnp.float32)
         o[:, pl.ds(pl.multiple_of(head * nope, nope), nope)] = (mixed * (1.0 / total)).astype(jnp.bfloat16)
 
     def attend_other(owners, js):
@@ -225,21 +267,26 @@
     def ring_step(s, fwd_right, fwd_left, before):
         from_left = device_at(place - s, core)
         from_right = device_at(place + s, core)
-        for j in range(heads):
-            go_right(from_left, j).wait_recv()
-            if j < fwd_right:
-                go_right(from_left, j).start()
-            go_across(from_left, j).start()
-            go_left(from_right, j).wait_recv()
-            if j >= fwd_left:
-                go_left(from_right, j).start()
-            go_across(from_right, j).start()
-            for owner in before:
-                go_across(owner, j).wait_recv()
-            attend(from_left, j)
-            attend(from_right, j)
-            for owner in before:
-                attend(owner, j)
+        for turn in range(2):
+            part_l = first_part(from_left) if turn == 0 else 1 - first_part(from_left)
+            part_r = first_part(from_right) if turn == 0 else 1 - first_part(from_right)
+            for j in range(heads):
+                go_right(from_left, j, part_l).wait_recv()
+                if j < fwd_right:
+                    go_right(from_left, j, part_l).start()
+                go_left(from_right, j, part_r).wait_recv()
+                if j >= fwd_left:
+                    go_left(from_right, j, part_r).start()
+                if turn == 0:
+                    for owner in before:
+                        go_across(owner, j).wait_recv()
+                    for owner in before:
+                        attend(owner, j)
+                else:
+                    go_across(from_left, j).start()
+                    go_across(from_right, j).start()
+                    attend(from_left, j)
+                    attend(from_right, j)
 
     def others(s):
         return (device_at(place - s, other_core), device_at(place + s, other_core))
@@ -266,18 +313,24 @@
         if j + half_right < heads:
             order.append(j + half_right)
     for j in order:
-        (go_right if j < half_right else go_left)(far, j).wait_recv()
-        go_across(far, j).start()
+        (go_right if j < half_right else go_left)(far, j, first_part(far)).wait_recv()
         for owner in last_before:
             go_across(owner, j).wait_recv()
         for owner in last_before:
             attend(owner, j)
+    for j in order:
+        (go_right if j < half_right else go_left)(far, j, 1 - first_part(far)).wait_recv()
+        go_across(far, j).start()
         attend(far, j)
     attend_other((far_other,), order)
 
-    @pl.loop(1, chips)
-    def _(d):
-        lat_out(d).wait_send()
+    @pl.loop(1, chips_half)
+    def _(i):
+        lat_out(near_chip(i)).wait_send()
+
+    @pl.loop(0, chips_half)
+    def _(i):
+        lat_out(far_chip(i)).wait_send()
 
     @pl.loop(0, chips)
     def _(d):
@@ -289,14 +342,16 @@
     @pl.loop(0, half - 1)
     def _(s):
         for j in range(heads):
-            go_right(device_at(place - s, core), j).wait_send()
-            go_left(device_at(place + s, core), j).wait_send()
+            for part in range(2):
+                go_right(device_at(place - s, core), j, part).wait_send()
+                go_left(device_at(place + s, core), j, part).wait_send()
 
     for j in range(heads):
-        if j < half_right:
-            go_right(device_at(place - (half - 1), core), j).wait_send()
-        else:
-            go_left(device_at(place + (half - 1), core), j).wait_send()
+        for part in range(2):
+            if j < half_right:
+                go_right(device_at(place - (half - 1), core), j, part).wait_send()
+            else:
+                go_left(device_at(place + (half - 1), core), j, part).wait_send()
 
 
 def on_device(grid_y, cores, queries, latents, w_key, w_value):
@@ -318,20 +373,20 @@
             pltpu.VMEM((devices, block, latents.shape[1]), jnp.bfloat16),
             pltpu.VMEM((heads, width, 2 * nope), jnp.bfloat16),
             pltpu.VMEM((2, rows, nope), jnp.bfloat16),
-            pltpu.VMEM((devices, heads, 2, rows, nope), jnp.bfloat16),
+            pltpu.VMEM((devices, heads, 2, 2, rows // 2, nope), jnp.bfloat16),
             dma((2 + 2 * heads,)),
             dma((devices,)),
             dma((chips,)),
             dma((devices,)),
-            dma((devices, heads)),
-            dma((devices, heads)),
-            dma((devices, heads)),
+            dma((devices, heads, 2)),
+            dma((devices, heads, 2)),
+            dma((devices, heads, 2)),
             dma((devices, heads)),
         ],
         compiler_params=pltpu.CompilerParams(
             collective_id=0, has_side_effects=True, vmem_limit_bytes=50 * 1024 * 1024
         ),
-    )(queries, latents, w_key, w_value)
+    )(*(pltpu.with_memory_space_constraint(a, pltpu.HBM) for a in (queries, latents, w_key, w_value)))
 
 
 def layout_of(mesh):

time: 64.1 us -> 60.7 us (0.947)
  local copies, waits for them, and re-layouts: 4.13 us -> 1.32 us
    unnamed x7 -> x1, local copies, waits for them, and re-layouts: 4.13 us -> 1.32 us
where the time goes in v3:
time: 60.7 us; the launch traced here: 60.5 us
  Pallas kernels  59.2 us (98%)
  local copies, waits for them, and re-layouts  1.32 us (2%)
    pallas_call x1, Pallas kernels, on_device(): pl.pallas_call(functools.partial(kernel, grid_y, cores), out_shape=jax.Sh...  59.2 us
    unnamed x1, local copies, waits for them, and re-layouts  1.32 us

profile of v3, /device:TPU:1, one launch (start us, length us, event | category | flops | bytes accessed | tf_op | source)
XLA Modules:
  0.0 60.5 jit_solution(15139500028710348680)
XLA Ops:
  0.0 59.2 %shard_map.46 = bf16[128,8192]{1,0:T(8,128)(2,1)S(1)} custom-call(bf16[128,12288]{1,0:T(8,128)(2,1)} %q_hbm.1, bf16[16,576]{1,0:T(8,128)(2,1)} %lat_hbm.1, bf16[4,512,128]{2,1,0:T(8,128)(2,1)} %wk_hbm.1, bf16[4,512,128]{2,1,0:T(8,128)(2,1)} %wv_hbm.1), custom_call_target="tpu_custom_call" | custom-call | tf_op jit(solution)/shard_map/pallas_call | solution.py:366
  59.2 1.3 %copy.6 = bf16[128,8192]{1,0:T(8,128)(2,1)} copy(bf16[128,8192]{1,0:T(8,128)(2,1)S(1)} %shard_map.46) | data formatting | bytes 4194304

commit v4 on v3

--- a/solution.py
+++ b/solution.py
@@ -77,7 +77,6 @@
         )
     for copy in w_copies:
         copy.start()
-    q_copy.start()
 
     barrier = pltpu.get_barrier_semaphore()
 
@@ -203,6 +202,7 @@
                     go_across(me, j - 1).start()
 
     project(near, False)
+    q_copy.start()
 
     @pl.loop(0, chips_half)
     def _(i):
@@ -253,13 +253,6 @@
         total = jnp.sum(weights, axis=1, keepdims=True)
         mixed = jnp.dot(weights.astype(jnp.bfloat16), values, preferred_element_type=jnp.float32)
         o[:, pl.ds(pl.multiple_of(head * nope, nope), nope)] = (mixed * (1.0 / total)).astype(jnp.bfloat16)
-
-    def attend_other(owners, js):
-        for j in js:
-            for owner in owners:
-                go_across(owner, j).wait_recv()
-            for owner in owners:
-                attend(owner, j)
 
     for j in range(heads):
         attend(me, j)
@@ -314,15 +307,19 @@
             order.append(j + half_right)
     for j in order:
         (go_right if j < half_right else go_left)(far, j, first_part(far)).wait_recv()
+        send(far, j, first_part(far), kv_right, across).start()
         for owner in last_before:
             go_across(owner, j).wait_recv()
         for owner in last_before:
             attend(owner, j)
     for j in order:
         (go_right if j < half_right else go_left)(far, j, 1 - first_part(far)).wait_recv()
-        go_across(far, j).start()
+        send(far, j, 1 - first_part(far), kv_right, across).start()
         attend(far, j)
-    attend_other((far_other,), order)
+    for j in order:
+        for part in range(2):
+            send(far_other, j, part, kv_right, across).wait_recv()
+        attend(far_other, j)
 
     @pl.loop(1, chips_half)
     def _(i):
@@ -336,8 +333,15 @@
     def _(d):
         owner = device_at(place + d, core)
         lat_on(owner).wait_send()
+
+    @pl.loop(half + 1, chips + half)
+    def _(d):
         for j in range(heads):
-            go_across(owner, j).wait_send()
+            go_across(device_at(place + d, core), j).wait_send()
+
+    for j in range(heads):
+        for part in range(2):
+            send(far, j, part, kv_right, across).wait_send()
 
     @pl.loop(0, half - 1)
     def _(s):

time: 60.7 us -> 60.8 us (level)
  no operation moved by 1% of the time
where the time goes in v4:
time: 60.8 us; the launch traced here: 60.7 us
  Pallas kernels  59.3 us (98%)
  local copies, waits for them, and re-layouts  1.32 us (2%)
    pallas_call x1, Pallas kernels, on_device(): pl.pallas_call(functools.partial(kernel, grid_y, cores), out_shape=jax.Sh...  59.3 us
    unnamed x1, local copies, waits for them, and re-layouts  1.32 us

profile of v4, /device:TPU:1, one launch (start us, length us, event | category | flops | bytes accessed | tf_op | source)
XLA Modules:
  0.0 60.7 jit_solution(4920663888861489260)
XLA Ops:
  0.0 59.3 %shard_map.46 = bf16[128,8192]{1,0:T(8,128)(2,1)S(1)} custom-call(bf16[128,12288]{1,0:T(8,128)(2,1)} %q_hbm.1, bf16[16,576]{1,0:T(8,128)(2,1)} %lat_hbm.1, bf16[4,512,128]{2,1,0:T(8,128)(2,1)} %wk_hbm.1, bf16[4,512,128]{2,1,0:T(8,128)(2,1)} %wv_hbm.1), custom_call_target="tpu_custom_call" | custom-call | tf_op jit(solution)/shard_map/pallas_call | solution.py:370
  59.4 1.3 %copy.6 = bf16[128,8192]{1,0:T(8,128)(2,1)} copy(bf16[128,8192]{1,0:T(8,128)(2,1)S(1)} %shard_map.46) | data formatting | bytes 4194304
